TPU v7x, 32 devices: a whole 2x2x4 slice. The times are simulated.
32 devices in a mesh: grp: 4 (over y, core), dev: 8 (over z, x).
Axes of the slice: x: 2, y: 2, z: 4, core: 2. Of those that a mesh axis runs over, the one named last changes fastest.
Arguments:
- densities: bfloat16 [32, 200, 200], P(('grp', 'dev')), may hold values from -0.4375 to 0.4375
- core_hamiltonian: bfloat16 [32, 200, 200], P(('grp', 'dev')), may hold values from -0.21875 to 0.21875
- embedding: bfloat16 [32, 200, 200], P(('grp', 'dev')), may hold values from -0.21875 to 0.21875
- fit_factors: bfloat16 [192, 200, 200], P('dev'), may hold values from -0.059814453 to 0.059814453
- orthogonalizers: bfloat16 [32, 200, 200], P(('grp', 'dev'))
- pairs: int32 [384, 2], replicated, may hold values from 0 to 31, as said below
- assignment: int32 [384], replicated, may hold values from 0 to 7, as said below
- owner_map: int32 [32], replicated, may hold values from 0 to 31, as said below
Outputs:
- slot_energies: float32 [768], P(('grp', 'dev'))
- total: float32 [], replicated
Inputs may be any that keep to these rules, and one draw needn't show every extreme that they name: `pairs`: dimer k belongs to group g = k // 96; its first fragment lies in block g, the fragments g * 8 to (g + 1) * 8 - 1, and its second fragment, different from the first, lies in block g or block g + 1 (only block g for the last group). `assignment`: no device receives more than 24 dimers of its group, and in every group some device receives exactly 24. `owner_map`: A permutation of the fragments that maps each block of 8 fragments onto the rows of the same block.
All inputs are finite; a program needn't handle non-finite values.
Results may differ from a plain program's by a relative error of at most 0.0003.
Values may be sent and summed in bfloat16 or wider, within the bound.
A program may use at most 128 MiB of HBM per device.

v0:
```python
import jax
import jax.numpy as jnp
from jax import lax
from jax.sharding import PartitionSpec as P

SLOTS = 24
F32 = jnp.float32
BF = jnp.bfloat16


def dot(left, right, dims=((1,), (0,))):
    return lax.dot_general(left, right, (dims, ((), ())), preferred_element_type=F32)


def lookup(table, mono, pairs, assignment, owner_map, group, member, members, groups):
    count = pairs.shape[0]
    per_group = count // groups
    rows = members * groups
    frag_ids = jnp.arange(rows, dtype=jnp.int32)
    row_of = lambda frag: jnp.sum(
        jnp.where(frag[:, None] == frag_ids[None, :], owner_map[None, :], 0), axis=1
    )
    first, second = (row_of(pairs[:, 0]), row_of(pairs[:, 1]))
    column = second - jnp.arange(count, dtype=jnp.int32) // per_group * members
    table_rows = jnp.sum(
        jnp.where((first[:, None] == frag_ids[None, :])[:, :, None], table[None, :, :], 0.0), axis=1
    )
    columns = jnp.arange(2 * members, dtype=jnp.int32)
    energies = jnp.sum(jnp.where(column[:, None] == columns[None, :], table_rows, 0.0), axis=1)
    energies = energies + jnp.sum(
        jnp.where(second[:, None] == frag_ids[None, :], mono[None, :], 0.0), axis=1
    )
    start = group * per_group
    mine = lax.dynamic_slice_in_dim(assignment, start, per_group, 0) == member
    mine_count = mine.astype(jnp.int32)
    before = jnp.cumsum(mine_count) - mine_count
    select = mine[None, :] & (before[None, :] == jnp.arange(SLOTS, dtype=jnp.int32)[:, None])
    own = lax.dynamic_slice_in_dim(energies, start, per_group, 0)
    return (jnp.sum(jnp.where(select, own[None, :], 0.0), axis=1), jnp.sum(energies))


def on_device(dens, core, embed, fit, ortho, pairs, assignment, owner_map):
    members, groups = (lax.axis_size("dev"), lax.axis_size("grp"))
    group, member = (lax.axis_index("grp"), lax.axis_index("dev"))
    basis = dens.shape[1]
    aux = fit.shape[0]
    flat_fit = fit.reshape(aux, basis * basis)
    gathered = lax.all_gather(dens, "dev", axis=0, tiled=True)
    coeffs = dot(gathered.reshape(members, basis * basis), flat_fit, ((1,), (1,))).astype(BF)
    coulomb = lax.psum_scatter(
        dot(coeffs, flat_fit).reshape(members, basis, basis).astype(BF),
        "dev",
        scatter_dimension=0,
        tiled=True,
    ).astype(F32)
    fock = (core.astype(F32) + embed.astype(F32) + coulomb).astype(BF)[0]
    d, x = (dens[0], ortho[0])
    v = dot(fock, x).astype(BF)
    u = dot(d, x).astype(BF)
    xf = dot(x, fock, ((0,), (0,))).astype(BF)
    xd = dot(x, d, ((0,), (0,))).astype(BF)
    a = dot(x, v, ((0,), (0,)))
    a_sym = (0.5 * (a + a.T)).astype(BF)
    ab = a.astype(BF)
    mono = (
        0.5 * jnp.trace(a)
        - 0.1875 * jnp.sum(a * a)
        + jnp.sum(dot(ab, ab) * dot(ab, ab, ((1,), (1,)))) / 256.0
        - jnp.sum(d.astype(F32) * fock.astype(F32))
    )
    block = jnp.stack([u, v, a_sym])[None]
    own_pool = lax.all_gather(block, "dev", axis=0, tiled=True)
    route = [(g, (g - 1) % groups) for g in range(groups)]
    next_pool = lax.ppermute(own_pool, "grp", route)
    pool = jnp.concatenate([own_pool, next_pool], axis=0)

    def pair_term(entry):
        u_j, v_j, c_sym = (entry[0], entry[1], entry[2])
        b = 0.5 * (dot(xf, u_j) + dot(xd, v_j))
        bb = b.astype(BF)
        left, right, gram = (dot(a_sym, bb), dot(bb, c_sym), dot(bb, bb, ((1,), (1,))))
        both = left + right
        quartic = left * left + right * right + both * both + gram * gram
        return jnp.sum(quartic / 128.0 - 0.375 * (b * b))

    terms = lax.map(pair_term, pool)
    line = jnp.concatenate([terms + mono, mono[None]])
    table = lax.all_gather(line[None], ("grp", "dev"), axis=0, tiled=True)
    return lookup(
        table[:, :-1], table[:, -1], pairs, assignment, owner_map, group, member, members, groups
    )


def solution(mesh):
    rows = P(("grp", "dev"), None, None)
    placed = (rows, rows, rows, P("dev", None, None), rows, P(), P(), P())
    return jax.shard_map(
        on_device, mesh=mesh, in_specs=placed, out_specs=(P(("grp", "dev")), P()), check_vma=False
    )
```

profile of v0, /device:TPU:0, one launch (start us, length us, event | category | flops | bytes accessed | tf_op | source)
XLA Modules:
  0.0 337.6 jit_solution(6582617387170707575)
XLA Ops:
  7.2 5.0 %reshape.89 = bf16[24,40000]{1,0:T(8,128)(2,1)} reshape(bf16[24,200,200]{2,1,0:T(8,128)(2,1)} %param.13) | data formatting | bytes 3840000 | tf_op jit(solution)/shard_map/reshape | solution.py:47
  12.2 6.2 %dot_general.53 = bf16[200,200,24]{1,0,2:T(8,128)(2,1)} reshape(bf16[40000,24]{0,1:T(8,128)(2,1)} %bitcast.123) | data formatting | bytes 3840000 | tf_op jit(solution)/shard_map/dot_general | solution.py:12
  18.4 36.1 %all_gather.9 = bf16[8,200,200]{2,1,0:T(8,128)(2,1)} all-gather(bf16[1,200,200]{2,1,0:T(8,128)(2,1)S(1)} %copy-done.2), channel_id=1, replica_groups=mesh['grp'=4,'dev'=8] {'dev'}, dimensions={0}, use_global_device_ids=true | all-gather | bytes 720000 | tf_op jit(solution)/shard_map/all_gather | solution.py:48
  54.5 3.9 %fusion.17 = bf16[8,200,200]{2,0,1:T(8,128)(2,1)S(1)} fusion(bf16[200,200,24]{1,0,2:T(8,128)(2,1)} %dot_general.53, bf16[24,200,200]{2,1,0:T(8,128)(2,1)S(1)} %copy-done.1, bf16[8,200,200]{2,1,0:T(8,128)(2,1)} %all_gather.9), kind=kOutput, calls=%fused_computation.24 | convolution fusion | flops 31040192 | bytes 5120000 | tf_op jit(solution)/shard_map/dot_general | solution.py:12
  59.7 58.7 %reduce-scatter.2.cloned.1.call-done = bf16[1,200,200]{2,1,0:T(8,128)(2,1)} async-done(((bf16[8,200,200]{2,1,0:T(8,128)(2,1)}), bf16[1,200,200]{2,1,0:T(8,128)(2,1)}) %reduce-scatter.2.cloned.1.call-update) | async-done | bytes 80016 | tf_op jit(solution)/shard_map/reduce_scatter | solution.py:50
  118.4 1.6 multiply_reduce_fusion
  122.0 52.0 %all-gather.4.cloned.1.call-done = bf16[24,200,200]{2,1,0:T(8,128)(2,1)} async-done(((bf16[3,200,200]{2,1,0:T(8,128)(2,1)}), bf16[24,200,200]{2,1,0:T(8,128)(2,1)}) %all-gather.4.cloned.1.call-update) | async-done | bytes 1920016 | tf_op jit(solution)/shard_map/all_gather | solution.py:72
  179.5 22.2 %collective-permute-done = bf16[8,3,200,200]{3,2,1,0:T(8,128)(2,1)S(1)} collective-permute-done((bf16[8,3,200,200]{3,2,1,0:T(8,128)(2,1)}, bf16[8,3,200,200]{3,2,1,0:T(8,128)(2,1)S(1)}, u32[]{:S(2)}, u32[]{:S(2)}) %collective-permute-start) | collective-permute-done | bytes 1920032 | tf_op jit(solution)/shard_map/ppermute | solution.py:74
  201.7 4.7 %pad_maximum_fusion = bf16[16,3,200,200]{3,2,1,0:T(8,128)(2,1)} fusion(bf16[8,3,200,200]{3,2,1,0:T(8,128)(2,1)S(1)} %collective-permute-done, bf16[8,3,200,200]{3,2,1,0:T(8,128)(2,1)} %bitcast.126), kind=kLoop, calls=%fused_computation.19 | loop fusion | flops 1920000 | bytes 7680000 | tf_op jit(solution)/shard_map/concatenate | solution.py:75
  206.4 82.9 %while.10 = (s32[]{:T(128)}, f32[16]{0:T(128)S(1)}, bf16[16,3,200,200]{3,2,1,0:T(8,128)(2,1)}, bf16[200,200]{1,0:T(8,128)(2,1)S(1)}, bf16[200,200]{1,0:T(8,128)(...) while((s32[]{:T(128)}, f32[16]{0:T(128)S(1)}, ...), condition=%wide.region_6.7_spmd, body=%wide.region_4.6_spmd.sunk | while | flops 80720000 | bytes 2147369 | solution.py:86
  207.5 1.1 fusion.94
  208.9 1.1 fusion.95
  211.6 1.1 fusion.93
  212.7 1.1 fusion.94
  214.0 1.1 fusion.95
  216.8 1.1 fusion.93
  217.9 1.1 fusion.94
  219.2 1.1 fusion.95
  222.0 1.1 fusion.93
  223.1 1.1 fusion.94
  224.4 1.1 fusion.95
  227.2 1.1 fusion.93
  228.3 1.1 fusion.94
  229.6 1.1 fusion.95
  233.5 1.1 fusion.94
  234.8 1.1 fusion.95
  238.6 1.1 fusion.94
  240.0 1.1 fusion.95
  242.7 1.1 fusion.93
  243.8 1.1 fusion.94
  245.2 1.1 fusion.95
  249.0 1.1 fusion.94
  250.3 1.1 fusion.95
  254.2 1.1 fusion.94
  255.5 1.1 fusion.95
  259.4 1.1 fusion.94
  260.7 1.1 fusion.95
  264.6 1.1 fusion.94
  265.9 1.1 fusion.95
  269.7 1.1 fusion.94
  271.1 1.1 fusion.95
  274.9 1.1 fusion.94
  276.2 1.1 fusion.95
  280.1 1.1 fusion.94
  281.4 1.1 fusion.95
  285.3 1.1 fusion.94
  286.6 1.1 fusion.95
  289.5 39.4 %all-reduce = f32[544]{0:T(1024)S(1)} all-reduce(f32[544]{0:T(1024)S(1)} %maximum_dynamic-update-slice_fusion), channel_id=3, replica_groups=mesh['grp'=4,'dev'=8] {'grp','dev'}, use_global_device_ids=true, to_apply=%add | all-reduce | flops 544 | bytes 4352
  (113 shorter events, 49.1 us)
Async XLA Ops:
  7.2 52.4 %copy-start = (bf16[1,200,200]{2,1,0:T(8,128)(2,1)S(1)}, bf16[1,200,200]{2,1,0:T(8,128)(2,1)}, u32[]{:S(2)}) copy-start(bf16[1,200,200]{2,1,0:T(8,128)(2,1)} %param.14) | copy-start | bytes 240004
  7.2 111.2 %reduce-scatter.2.cloned.1.call-start = ((), (), s32[]{:S(2)}) async-start(), calls=%async_computation.1 | async-start | bytes 921600 | tf_op jit(solution)/shard_map/reduce_scatter | solution.py:50
  12.2 6.2 %copy-start.2 = (bf16[1,200,200]{2,1,0:T(8,128)(2,1)S(1)}, bf16[1,200,200]{2,1,0:T(8,128)(2,1)}, u32[]{:S(2)}) copy-start(bf16[1,200,200]{2,1,0:T(8,128)(2,1)} %param.10) | copy-start | bytes 240004
  12.2 42.3 %copy-start.1 = (bf16[24,200,200]{2,1,0:T(8,128)(2,1)S(1)}, bf16[24,200,200]{2,1,0:T(8,128)(2,1)}, u32[]{:S(2)}) copy-start(bf16[24,200,200]{2,1,0:T(8,128)(2,1)} %param.13) | copy-start | bytes 5760004
  58.4 60.1 %copy-start.4 = (bf16[1,200,200]{2,1,0:T(8,128)(2,1)S(1)}, bf16[1,200,200]{2,1,0:T(8,128)(2,1)}, u32[]{:S(2)}) copy-start(bf16[1,200,200]{2,1,0:T(8,128)(2,1)} %param.12) | copy-start | bytes 240004
  58.4 60.0 %copy-start.5 = (bf16[1,200,200]{2,1,0:T(8,128)(2,1)S(1)}, bf16[1,200,200]{2,1,0:T(8,128)(2,1)}, u32[]{:S(2)}) copy-start(bf16[1,200,200]{2,1,0:T(8,128)(2,1)} %param.11) | copy-start | bytes 240004
  59.4 115.7 %copy-start.6 = (s32[384,2]{0,1:T(2,128)S(1)}, s32[384,2]{0,1:T(2,128)}, u32[]{:S(2)}) copy-start(s32[384,2]{0,1:T(2,128)} %param.15) | copy-start | bytes 9220
  59.4 115.7 %copy-start.7 = (s32[32]{0:T(128)S(1)}, s32[32]{0:T(128)}, u32[]{:S(2)}) copy-start(s32[32]{0:T(128)} %param.17) | copy-start | bytes 388
  59.5 115.9 %copy-start.3 = (bf16[1,200,200]{2,1,0:T(8,128)(2,1)S(1)}, bf16[1,200,200]{2,1,0:T(8,128)(2,1)}, u32[]{:S(2)}) copy-start(bf16[1,200,200]{2,1,0:T(8,128)(2,1)} %param.10) | copy-start | bytes 240004
  59.5 114.5 %all-gather.4.cloned.1.call-start = ((), (), s32[]{:S(2)}) async-start(), calls=%async_computation.2 | async-start | bytes 2764800 | tf_op jit(solution)/shard_map/all_gather | solution.py:72
  174.0 27.7 %collective-permute-start = (bf16[8,3,200,200]{3,2,1,0:T(8,128)(2,1)}, bf16[8,3,200,200]{3,2,1,0:T(8,128)(2,1)S(1)}, u32[]{:S(2)}, u32[]{:S(2)}) collective-permute-start(bf16[8,3,200,200]{3,2,1,0:T(8,128)(2,1)} %bitcast.125), channel_id=1, source_target_pairs={{0,24},{8,0},{16,8},{24,16},{1,25},{9,1},{17,9},{25,17},{2,26},{10... | collective-permute-start | bytes 5760008 | tf_op jit(solution)/shard_map/ppermute | solution.py:74
Sparse Core Ops, SparseCore 0:
  59.6 58.7 reduce-scatter.1
  122.2 51.7 all-gather.3
where the time goes:
time: 340 us; the launch traced here: 338 us
  waiting for transfers between devices  133 us (39%)
  matrix products  76.3 us (22%)
  blocking collectives  75.5 us (22%)
  local copies, waits for them, and re-layouts  25 us (7%)
  between operations  16.9 us (5%)
  other arithmetic  10.5 us (3%)
    dot_general x88, matrix products, dot(): lax.dot_general(left, right, (dims, ((), ())), preferred_element_type=F32)  76.3 us
    reduce_scatter x1, waiting for transfers between devices, on_device(): lax.psum_scatter(dot(coeffs, flat_fit).reshape(members, basis, basis).ast...  58.7 us
    all_gather x1, waiting for transfers between devices, on_device(): own_pool = lax.all_gather(block, 'dev', axis=0, tiled=True)  52 us
    unnamed x1, blocking collectives  39.4 us
    all_gather x1, blocking collectives, on_device(): gathered = lax.all_gather(dens, 'dev', axis=0, tiled=True)  36.1 us
    ppermute x1, waiting for transfers between devices, on_device(): next_pool = lax.ppermute(own_pool, 'grp', route)  22.2 us
    dynamic_update_slice x16, local copies, waits for them, and re-layouts, on_device(): terms = lax.map(pair_term, pool)  12.1 us
  transfers between devices with their start and end apart: 3, of which 3 were waited for; matrix products, arithmetic and copies ran while one was open for 1% of the time, Pallas kernels for 0%

commit v1 on v0

--- a/solution.py
+++ b/solution.py
@@ -45,7 +45,12 @@
     basis = dens.shape[1]
     aux = fit.shape[0]
     flat_fit = fit.reshape(aux, basis * basis)
-    gathered = lax.all_gather(dens, "dev", axis=0, tiled=True)
+    ring = [dens]
+    for hop in range(7):
+        ring.append(lax.ppermute(ring[-1], "dev", [(dev, (dev + 1) % 8) for dev in range(8)]))
+    gathered = jnp.roll(
+        jnp.concatenate(ring[::-1], axis=0), (lax.axis_index("dev") + 1) * ring[0].shape[0], axis=0
+    )
     coeffs = dot(gathered.reshape(members, basis * basis), flat_fit, ((1,), (1,))).astype(BF)
     coulomb = lax.psum_scatter(
         dot(coeffs, flat_fit).reshape(members, basis, basis).astype(BF),

time: 340 us -> 370 us (1.088)
  waiting for transfers between devices: 133 us -> 185 us
  blocking collectives: 75.5 us -> 39.4 us
  local copies, waits for them, and re-layouts: 25 us -> 35.7 us
    ppermute x0 -> x7, waiting for transfers between devices: none -> 51.9 us  [on_device(): lax.ppermute(ring[-1], 'dev', [(dev, (dev + 1) % 8) for dev in range(8)])]
    all_gather x1 -> x0, blocking collectives: 36.1 us -> none  [on_device(): gathered = lax.all_gather(dens, 'dev', axis=0, tiled=True)]
    concatenate x0 -> x1, local copies, waits for them, and re-layouts: none -> 11.1 us  [on_device(): jnp.roll(jnp.concatenate(ring[::-1], axis=0), (lax.axis_index('dev') + 1)...]
  transfers between devices with their start and end apart: 3 -> 10, of which waited for: 3 -> 9; matrix products, arithmetic and copies ran while one was open for 1% -> 3% of each run, Pallas kernels for 0% -> 0%
where the time goes in v1:
time: 370 us; the launch traced here: 368 us
  waiting for transfers between devices  185 us (50%)
  matrix products  76.6 us (21%)
  blocking collectives  39.4 us (11%)
  local copies, waits for them, and re-layouts  35.7 us (10%)
  between operations  16.9 us (5%)
  other arithmetic  10.6 us (3%)
    dot_general x88, matrix products, dot(): lax.dot_general(left, right, (dims, ((), ())), preferred_element_type=F32)  76.6 us
    reduce_scatter x1, waiting for transfers between devices, on_device(): lax.psum_scatter(dot(coeffs, flat_fit).reshape(members, basis, basis).ast...  59.3 us
    all_gather x1, waiting for transfers between devices, on_device(): own_pool = lax.all_gather(block, 'dev', axis=0, tiled=True)  52 us
    ppermute x7, waiting for transfers between devices, on_device(): lax.ppermute(ring[-1], 'dev', [(dev, (dev + 1) % 8) for dev in range(8)])  51.9 us
    unnamed x1, blocking collectives  39.4 us
    ppermute x1, waiting for transfers between devices, on_device(): next_pool = lax.ppermute(own_pool, 'grp', route)  22.2 us
    dynamic_update_slice x16, local copies, waits for them, and re-layouts, on_device(): terms = lax.map(pair_term, pool)  12.1 us
    concatenate x1, local copies, waits for them, and re-layouts, on_device(): jnp.roll(jnp.concatenate(ring[::-1], axis=0), (lax.axis_index('dev') + 1)...  11.1 us
  transfers between devices with their start and end apart: 10, of which 9 were waited for; matrix products, arithmetic and copies ran while one was open for 3% of the time, Pallas kernels for 0%

profile of v1, /device:TPU:0, one launch (start us, length us, event | category | flops | bytes accessed | tf_op | source)
XLA Modules:
  0.0 368.0 jit_solution(4242649312820011897)
XLA Ops:
  8.3 3.0 collective-permute-start
  11.3 8.1 %collective-permute-done = bf16[1,200,200]{2,0,1:T(2,128)(2,1)S(1)} collective-permute-done((bf16[1,200,200]{2,0,1:T(2,128)(2,1)S(1)}, bf16[1,200,200]{2,0,1:T(2,128)(2,1)S(1)}, u32[]{:S(2)}, u32[]{:S(2)}) %collective-permute-start) | collective-permute-done | bytes 80032 | tf_op jit(solution)/shard_map/ppermute | solution.py:50
  19.4 8.9 %collective-permute-done.1 = bf16[1,200,200]{2,0,1:T(2,128)(2,1)S(1)} collective-permute-done((bf16[1,200,200]{2,0,1:T(2,128)(2,1)S(1)}, bf16[1,200,200]{2,0,1:T(2,128)(2,1)S(1)}, u32[]{:S(2)}, u32[]{:S(2)}) %collective-permute-start.1) | collective-permute-done | bytes 80032 | tf_op jit(solution)/shard_map/ppermute | solution.py:50
  28.4 8.5 %collective-permute-done.2 = bf16[1,200,200]{2,0,1:T(2,128)(2,1)S(1)} collective-permute-done((bf16[1,200,200]{2,0,1:T(2,128)(2,1)S(1)}, bf16[1,200,200]{2,0,1:T(2,128)(2,1)S(1)}, u32[]{:S(2)}, u32[]{:S(2)}) %collective-permute-start.2) | collective-permute-done | bytes 80032 | tf_op jit(solution)/shard_map/ppermute | solution.py:50
  36.8 8.6 %collective-permute-done.3 = bf16[1,200,200]{2,0,1:T(2,128)(2,1)} collective-permute-done((bf16[1,200,200]{2,0,1:T(2,128)(2,1)S(1)}, bf16[1,200,200]{2,0,1:T(2,128)(2,1)}, u32[]{:S(2)}, u32[]{:S(2)}) %collective-permute-start.3) | collective-permute-done | bytes 80032 | tf_op jit(solution)/shard_map/ppermute | solution.py:50
  45.4 8.7 %collective-permute-done.4 = bf16[1,200,200]{2,0,1:T(2,128)(2,1)S(1)} collective-permute-done((bf16[1,200,200]{2,0,1:T(2,128)(2,1)}, bf16[1,200,200]{2,0,1:T(2,128)(2,1)S(1)}, u32[]{:S(2)}, u32[]{:S(2)}) %collective-permute-start.4) | collective-permute-done | bytes 80032 | tf_op jit(solution)/shard_map/ppermute | solution.py:50
  54.7 9.1 %collective-permute-done.5 = bf16[1,200,200]{2,0,1:T(2,128)(2,1)} collective-permute-done((bf16[1,200,200]{2,0,1:T(2,128)(2,1)S(1)}, bf16[1,200,200]{2,0,1:T(2,128)(2,1)}, u32[]{:S(2)}, u32[]{:S(2)}) %collective-permute-start.5) | collective-permute-done | bytes 80032 | tf_op jit(solution)/shard_map/ppermute | solution.py:50
  63.9 3.9 %reshape.89 = bf16[24,40000]{1,0:T(8,128)(2,1)S(1)} reshape(bf16[24,200,200]{2,1,0:T(8,128)(2,1)} %param.13) | data formatting | bytes 3840000 | tf_op jit(solution)/shard_map/reshape | solution.py:47
  67.8 5.0 %dot_general.53 = bf16[200,200,24]{1,0,2:T(8,128)(2,1)} reshape(bf16[40000,24]{0,1:T(8,128)(2,1)S(1)} %bitcast.123) | data formatting | bytes 3840000 | tf_op jit(solution)/shard_map/dot_general | solution.py:12
  72.8 11.1 %concatenate.12 = bf16[16,200,200]{2,0,1:T(8,128)(2,1)} concatenate(bf16[1,200,200]{2,0,1:T(2,128)(2,1)} %collective-permute-done.6, bf16[1,200,200]{2,0,1:T(2,128)(2,1)} %collective-permute-done.5, bf16[1,200,200]{2,0,1:T(2,128)(2,1)} %copy-done.3, bf16[1,200,200]{2,0,1:T(2,128)(2,1)} %collective-permute-done.3, bf16[1,200,200]{2,0,1:T(2,128)(2,1)S(1)} %collective-permute-done.2, ...), dimensions={0} | concatenate | bytes 2560000 | tf_op jit(solution)/shard_map/jit(_roll_dynamic)/concatenate | solution.py:51
  84.0 4.1 %fusion.17 = bf16[8,200,200]{2,0,1:T(8,128)(2,1)S(1)} fusion(bf16[200,200,24]{1,0,2:T(8,128)(2,1)} %dot_general.53, bf16[24,200,200]{2,1,0:T(8,128)(2,1)S(1)} %copy-done.1, bf16[16,200,200]{2,0,1:T(8,128)(2,1)} %concatenate.12, s32[]{:T(128)S(6)} %select_n.59), kind=kOutput, calls=%fused_computation.24 | convolution fusion | flops 31040192 | bytes 5836804 | tf_op jit(solution)/shard_map/dot_general | solution.py:12
  89.5 59.3 %reduce-scatter.2.cloned.1.call-done = bf16[1,200,200]{2,1,0:T(8,128)(2,1)} async-done(((bf16[8,200,200]{2,1,0:T(8,128)(2,1)}), bf16[1,200,200]{2,1,0:T(8,128)(2,1)}) %reduce-scatter.2.cloned.1.call-update) | async-done | bytes 80016 | tf_op jit(solution)/shard_map/reduce_scatter | solution.py:55
  148.8 1.6 multiply_reduce_fusion
  152.4 52.0 %all-gather.4.cloned.1.call-done = bf16[24,200,200]{2,1,0:T(8,128)(2,1)} async-done(((bf16[3,200,200]{2,1,0:T(8,128)(2,1)}), bf16[24,200,200]{2,1,0:T(8,128)(2,1)}) %all-gather.4.cloned.1.call-update) | async-done | bytes 1920016 | tf_op jit(solution)/shard_map/all_gather | solution.py:77
  209.9 22.2 %collective-permute-done.7 = bf16[8,3,200,200]{3,2,1,0:T(8,128)(2,1)S(1)} collective-permute-done((bf16[8,3,200,200]{3,2,1,0:T(8,128)(2,1)}, bf16[8,3,200,200]{3,2,1,0:T(8,128)(2,1)S(1)}, u32[]{:S(2)}, u32[]{:S(2)}) %collective-permute-start.7) | collective-permute-done | bytes 1920032 | tf_op jit(solution)/shard_map/ppermute | solution.py:79
  232.1 4.7 %pad_maximum_fusion = bf16[16,3,200,200]{3,2,1,0:T(8,128)(2,1)} fusion(bf16[8,3,200,200]{3,2,1,0:T(8,128)(2,1)S(1)} %collective-permute-done.7, bf16[8,3,200,200]{3,2,1,0:T(8,128)(2,1)} %bitcast.126), kind=kLoop, calls=%fused_computation.19 | loop fusion | flops 1920000 | bytes 7680000 | tf_op jit(solution)/shard_map/concatenate | solution.py:80
  236.8 82.9 %while.10 = (s32[]{:T(128)}, f32[16]{0:T(128)S(1)}, bf16[16,3,200,200]{3,2,1,0:T(8,128)(2,1)}, bf16[200,200]{1,0:T(8,128)(2,1)S(1)}, bf16[200,200]{1,0:T(8,128)(...) while((s32[]{:T(128)}, f32[16]{0:T(128)S(1)}, ...), condition=%wide.region_6.7_spmd, body=%wide.region_4.6_spmd.sunk | while | flops 80720000 | bytes 2147369 | solution.py:91
  237.9 1.1 fusion.96
  239.2 1.1 fusion.97
  243.1 1.1 fusion.96
  244.4 1.1 fusion.97
  248.3 1.1 fusion.96
  249.6 1.1 fusion.97
  253.4 1.1 fusion.96
  254.8 1.1 fusion.97
  258.6 1.1 fusion.96
  259.9 1.1 fusion.97
  263.8 1.1 fusion.96
  265.1 1.1 fusion.97
  269.0 1.1 fusion.96
  270.3 1.1 fusion.97
  274.2 1.1 fusion.96
  275.5 1.1 fusion.97
  279.3 1.1 fusion.96
  280.7 1.1 fusion.97
  284.5 1.1 fusion.96
  285.9 1.1 fusion.97
  289.7 1.1 fusion.96
  291.0 1.1 fusion.97
  294.9 1.1 fusion.96
  296.2 1.1 fusion.97
  300.1 1.1 fusion.96
  301.4 1.1 fusion.97
  306.6 1.1 fusion.97
  311.8 1.1 fusion.97
  315.6 1.1 fusion.96
  316.9 1.1 fusion.97
  319.9 39.4 %all-reduce = f32[544]{0:T(1024)S(1)} all-reduce(f32[544]{0:T(1024)S(1)} %maximum_dynamic-update-slice_fusion), channel_id=3, replica_groups=mesh['grp'=4,'dev'=8] {'grp','dev'}, use_global_device_ids=true, to_apply=%add | all-reduce | flops 544 | bytes 4352
  (128 shorter events, 58.6 us)
Async XLA Ops:
  7.2 82.1 %copy-start = (bf16[1,200,200]{2,1,0:T(8,128)(2,1)S(1)}, bf16[1,200,200]{2,1,0:T(8,128)(2,1)}, u32[]{:S(2)}) copy-start(bf16[1,200,200]{2,1,0:T(8,128)(2,1)} %param.14) | copy-start | bytes 240004
  7.2 141.6 %reduce-scatter.2.cloned.1.call-start = ((), (), s32[]{:S(2)}) async-start(), calls=%async_computation.1 | async-start | bytes 921600 | tf_op jit(solution)/shard_map/reduce_scatter | solution.py:55
  8.3 11.1 %collective-permute-start = (bf16[1,200,200]{2,0,1:T(2,128)(2,1)S(1)}, bf16[1,200,200]{2,0,1:T(2,128)(2,1)S(1)}, u32[]{:S(2)}, u32[]{:S(2)}) collective-permute-start(bf16[1,200,200]{2,0,1:T(2,128)(2,1)S(1)} %copy.67), channel_id=1, source_target_pairs={{0,1},{1,2},{2,3},{3,4},{4,5},{5,6},{6,7},{7,0},{8,9},{9,10},{10,1... | collective-permute-start | bytes 240008 | tf_op jit(solution)/shard_map/ppermute | solution.py:50
  19.4 8.9 %collective-permute-start.1 = (bf16[1,200,200]{2,0,1:T(2,128)(2,1)S(1)}, bf16[1,200,200]{2,0,1:T(2,128)(2,1)S(1)}, u32[]{:S(2)}, u32[]{:S(2)}) collective-permute-start(bf16[1,200,200]{2,0,1:T(2,128)(2,1)S(1)} %collective-permute-done), channel_id=1, source_target_pairs={{0,1},{1,2},{2,3},{3,4},{4,5},{5,6},{6,7},{7,0},{8,9},{9,10},{10,1... | collective-permute-start | bytes 240008 | tf_op jit(solution)/shard_map/ppermute | solution.py:50
  28.4 8.5 %collective-permute-start.2 = (bf16[1,200,200]{2,0,1:T(2,128)(2,1)S(1)}, bf16[1,200,200]{2,0,1:T(2,128)(2,1)S(1)}, u32[]{:S(2)}, u32[]{:S(2)}) collective-permute-start(bf16[1,200,200]{2,0,1:T(2,128)(2,1)S(1)} %collective-permute-done.1), channel_id=1, source_target_pairs={{0,1},{1,2},{2,3},{3,4},{4,5},{5,6},{6,7},{7,0},{8,9},{9,10},{10,1... | collective-permute-start | bytes 240008 | tf_op jit(solution)/shard_map/ppermute | solution.py:50
  36.8 8.6 %collective-permute-start.3 = (bf16[1,200,200]{2,0,1:T(2,128)(2,1)S(1)}, bf16[1,200,200]{2,0,1:T(2,128)(2,1)}, u32[]{:S(2)}, u32[]{:S(2)}) collective-permute-start(bf16[1,200,200]{2,0,1:T(2,128)(2,1)S(1)} %collective-permute-done.2), channel_id=1, source_target_pairs={{0,1},{1,2},{2,3},{3,4},{4,5},{5,6},{6,7},{7,0},{8,9},{9,10},{10,1... | collective-permute-start | bytes 240008 | tf_op jit(solution)/shard_map/ppermute | solution.py:50
  45.4 8.7 %collective-permute-start.4 = (bf16[1,200,200]{2,0,1:T(2,128)(2,1)}, bf16[1,200,200]{2,0,1:T(2,128)(2,1)S(1)}, u32[]{:S(2)}, u32[]{:S(2)}) collective-permute-start(bf16[1,200,200]{2,0,1:T(2,128)(2,1)} %collective-permute-done.3), channel_id=1, source_target_pairs={{0,1},{1,2},{2,3},{3,4},{4,5},{5,6},{6,7},{7,0},{8,9},{9,10},{10,1... | collective-permute-start | bytes 240008 | tf_op jit(solution)/shard_map/ppermute | solution.py:50
  54.0 0.7 copy-start.3
  54.7 9.1 %collective-permute-start.5 = (bf16[1,200,200]{2,0,1:T(2,128)(2,1)S(1)}, bf16[1,200,200]{2,0,1:T(2,128)(2,1)}, u32[]{:S(2)}, u32[]{:S(2)}) collective-permute-start(bf16[1,200,200]{2,0,1:T(2,128)(2,1)S(1)} %collective-permute-done.4), channel_id=1, source_target_pairs={{0,1},{1,2},{2,3},{3,4},{4,5},{5,6},{6,7},{7,0},{8,9},{9,10},{10,1... | collective-permute-start | bytes 240008 | tf_op jit(solution)/shard_map/ppermute | solution.py:50
  63.9 9.0 %collective-permute-start.6 = (bf16[1,200,200]{2,0,1:T(2,128)(2,1)}, bf16[1,200,200]{2,0,1:T(2,128)(2,1)}, u32[]{:S(2)}, u32[]{:S(2)}) collective-permute-start(bf16[1,200,200]{2,0,1:T(2,128)(2,1)} %collective-permute-done.5), channel_id=1, source_target_pairs={{0,1},{1,2},{2,3},{3,4},{4,5},{5,6},{6,7},{7,0},{8,9},{9,10},{10,1... | collective-permute-start | bytes 240008 | tf_op jit(solution)/shard_map/ppermute | solution.py:50
  72.8 11.1 %copy-start.1 = (bf16[24,200,200]{2,1,0:T(8,128)(2,1)S(1)}, bf16[24,200,200]{2,1,0:T(8,128)(2,1)}, u32[]{:S(2)}) copy-start(bf16[24,200,200]{2,1,0:T(8,128)(2,1)} %param.13) | copy-start | bytes 5760004
  88.1 1.2 copy-start.2
  88.1 60.6 %copy-start.4 = (bf16[1,200,200]{2,1,0:T(8,128)(2,1)S(1)}, bf16[1,200,200]{2,1,0:T(8,128)(2,1)}, u32[]{:S(2)}) copy-start(bf16[1,200,200]{2,1,0:T(8,128)(2,1)} %param.12) | copy-start | bytes 240004
  88.1 60.6 %copy-start.5 = (bf16[1,200,200]{2,1,0:T(8,128)(2,1)S(1)}, bf16[1,200,200]{2,1,0:T(8,128)(2,1)}, u32[]{:S(2)}) copy-start(bf16[1,200,200]{2,1,0:T(8,128)(2,1)} %param.11) | copy-start | bytes 240004
  89.2 116.3 %copy-start.6 = (s32[384,2]{0,1:T(2,128)S(1)}, s32[384,2]{0,1:T(2,128)}, u32[]{:S(2)}) copy-start(s32[384,2]{0,1:T(2,128)} %param.15) | copy-start | bytes 9220
  89.2 116.3 %copy-start.7 = (s32[32]{0:T(128)S(1)}, s32[32]{0:T(128)}, u32[]{:S(2)}) copy-start(s32[32]{0:T(128)} %param.17) | copy-start | bytes 388
  89.2 115.1 %all-gather.4.cloned.1.call-start = ((), (), s32[]{:S(2)}) async-start(), calls=%async_computation.2 | async-start | bytes 2764800 | tf_op jit(solution)/shard_map/all_gather | solution.py:77
  204.4 27.7 %collective-permute-start.7 = (bf16[8,3,200,200]{3,2,1,0:T(8,128)(2,1)}, bf16[8,3,200,200]{3,2,1,0:T(8,128)(2,1)S(1)}, u32[]{:S(2)}, u32[]{:S(2)}) collective-permute-start(bf16[8,3,200,200]{3,2,1,0:T(8,128)(2,1)} %bitcast.125), channel_id=1, source_target_pairs={{0,24},{8,0},{16,8},{24,16},{1,25},{9,1},{17,9},{25,17},{2,26},{10... | collective-permute-start | bytes 5760008 | tf_op jit(solution)/shard_map/ppermute | solution.py:79
Sparse Core Ops, SparseCore 0:
  89.4 59.3 reduce-scatter.1
  152.5 51.7 all-gather.3
